TPU v7x, 256 devices: a whole 4x4x8 slice. The times are simulated.
256 devices in a mesh: gx: 2 (over core), gy: 4 (over x), gz: 32 (over z, y).
Axes of the slice: x: 4, y: 4, z: 8, core: 2. Of those that a mesh axis runs over, the one named last changes fastest.
Arguments:
- resid_x: float32 [6, 8, 32, 120, 512], P('gx', 'gy', 'gz'), may hold values from -6 to 6
- resid_y: float32 [4, 12, 32, 120, 512], P('gx', 'gy', 'gz'), may hold values from -6 to 6
- face_weights: float32 [4, 8, 32, 4, 120], P('gx', 'gy', 'gz'), may hold values from 0.25 to 0.75
- face_counts: int32 [4, 8, 32, 4], P('gx', 'gy', 'gz'), may hold values from 1 to 4, as said below
- neumann: bfloat16 [4, 8, 32, 480, 480], P('gx', 'gy', 'gz'), may hold values from -0.25 to 0.25
- schur: bfloat16 [4, 8, 32, 480, 480], P('gx', 'gy', 'gz'), may hold values from -0.25 to 0.25
- basis: bfloat16 [4, 8, 32, 480, 64], P('gx', 'gy', 'gz'), may hold values from -0.25 to 0.25
- coarse_map: int32 [4, 8, 32, 64], P('gx', 'gy', 'gz'), may hold values from 0 to 511
- column_inverse: float32 [2, 4, 512, 512], P('gx', 'gy', 'gz'), may hold values from -0.25 to 0.25
- column_basis: float32 [2, 4, 512, 512], P('gx', 'gy', 'gz'), may hold values from -0.25 to 0.25
- top_inverse: float32 [512, 512], replicated, may hold values from -0.09375 to 0.09375
Outputs:
- z_x: float32 [6, 8, 32, 120, 512], P('gx', 'gy', 'gz')
- z_y: float32 [4, 12, 32, 120, 512], P('gx', 'gy', 'gz')
- schur_image: bfloat16 [4, 8, 32, 480, 512], P('gx', 'gy', 'gz')
Inputs may be any that keep to these rules, and one draw needn't show every extreme that they name: `face_counts`: only the first 30 * count of a face's 120 dofs are live; about one face in eight has 4 live mesh faces. `coarse_map`: several local coarse dofs may share a column coarse dof.
All inputs are finite; a program needn't handle non-finite values.
Results may differ from a plain program's by a relative error of at most 0.0063.
Values sent between devices are 32-bit elements; how exact they have to be, the bound alone decides.
No kernel may reach another device: no remote copies, remote signals or barrier semaphores. Data moves between devices by JAX's collectives and lax.ppermute only.
A program may use at most 64 MiB of HBM per device.

v0:
```python
import jax
import jax.numpy as jnp
from jax import lax
from jax.sharding import PartitionSpec as P

BLK = 30


def with_halo(array, sides, width):
    for axis, dim in sides:
        size, length = (lax.axis_size(axis), array.shape[dim])
        up = [(i, (i + 1) % size) for i in range(size)]
        down = [(j, i) for i, j in up]
        last = lax.slice_in_dim(array, length - width, length, axis=dim)
        initial = lax.slice_in_dim(array, 0, width, axis=dim)
        before = lax.ppermute(last, axis, up)
        after = lax.ppermute(initial, axis, down)
        array = jnp.concatenate([before, array, after], axis=dim)
    return array


def assemble_x(copies):
    padded = with_halo(copies, (("gx", 0),), 1)
    return copies + jnp.stack([padded[0], jnp.zeros_like(padded[0]), padded[4]], 0)


def assemble_y(copies):
    padded = with_halo(copies, (("gy", 1),), 1)
    return copies + jnp.stack([padded[:, 0], jnp.zeros_like(padded[:, 0]), padded[:, 4]], 1)


def gather_faces(along_x, along_y):
    return jnp.stack([along_x[0:2], along_x[1:3], along_y[:, 0:2], along_y[:, 1:3]], 2)


def on_device(
    resid_x,
    resid_y,
    face_weights,
    face_counts,
    neumann,
    schur,
    basis,
    coarse_map,
    column_inverse,
    column_basis,
    top_inverse,
):
    high = lax.Precision.HIGHEST
    face_dofs = resid_x.shape[3]
    loads = resid_x.shape[4]
    inner = neumann.shape[3]
    coarse_local = basis.shape[4]
    column_size = column_inverse.shape[3]
    dof_index = jnp.arange(face_dofs, dtype=jnp.int32)
    live = (dof_index[None, None, None, :] < face_counts[:, :, 0, :, None] * BLK).astype(
        jnp.float32
    )
    scale = face_weights[:, :, 0] * live
    assembled_x = assemble_x(resid_x)[:, :, 0]
    assembled_y = assemble_y(resid_y)[:, :, 0]
    faces = gather_faces(assembled_x, assembled_y)
    upart = (faces * scale[..., None]).reshape(4, inner, loads).astype(jnp.bfloat16)
    neumann_flat = neumann.reshape(4, inner, inner)
    basis_flat = basis.reshape(4, inner, coarse_local)
    wpart = jnp.einsum("snk,skr->snr", neumann_flat, upart, preferred_element_type=jnp.float32)
    gpart = jnp.einsum("snc,snr->scr", basis_flat, upart, preferred_element_type=jnp.float32)
    targets = coarse_map.reshape(4 * coarse_local)
    onehot = (targets[:, None] == jnp.arange(column_size, dtype=jnp.int32)[None, :]).astype(
        jnp.float32
    )
    column_part = lax.dot_general(
        onehot, gpart.reshape(4 * coarse_local, loads), (((0,), (0,)), ((), ())), precision=high
    )
    column_res = lax.psum(column_part, "gz")
    inverse_rows = column_inverse[0, 0]
    basis_rows = column_basis[0, 0]
    row_count = inverse_rows.shape[0]
    row_start = lax.axis_index("gz") * row_count
    own_rows = lax.dynamic_slice_in_dim(column_res, row_start, row_count, 0)
    level_two = jnp.dot(inverse_rows, column_res, precision=high)
    top_part = lax.dot_general(basis_rows, own_rows, (((0,), (0,)), ((), ())), precision=high)
    column_top = lax.psum(top_part, "gz")
    top_res = lax.psum(column_top, ("gx", "gy"))
    level_three = jnp.dot(top_inverse, top_res, precision=high)
    value_rows = level_two + jnp.dot(basis_rows, level_three, precision=high)
    column_vals = lax.all_gather(value_rows, "gz", axis=0, tiled=True)
    coarse_vals = (
        jnp.dot(onehot, column_vals, precision=high)
        .reshape(4, coarse_local, loads)
        .astype(jnp.bfloat16)
    )
    ypart = wpart + jnp.einsum(
        "snc,scr->snr", basis_flat, coarse_vals, preferred_element_type=jnp.float32
    )
    contrib = ypart.reshape(2, 2, 4, face_dofs, loads) * scale[..., None]
    send_x = jnp.stack(
        [contrib[0, :, 0], contrib[0, :, 1] + contrib[1, :, 0], contrib[1, :, 1]], 0
    )[:, :, None]
    send_y = jnp.stack(
        [contrib[:, 0, 2], contrib[:, 0, 3] + contrib[:, 1, 2], contrib[:, 1, 3]], 1
    )[:, :, None]
    z_x = assemble_x(send_x)
    z_y = assemble_y(send_y)
    zfaces = gather_faces(z_x[:, :, 0], z_y[:, :, 0])
    zsub = (zfaces * live[..., None]).reshape(4, inner, loads).astype(jnp.bfloat16)
    image = jnp.einsum(
        "snk,skr->snr", schur.reshape(4, inner, inner), zsub, preferred_element_type=jnp.float32
    )
    return (z_x, z_y, image.astype(jnp.bfloat16).reshape(2, 2, 1, inner, loads))


def solution(mesh):
    return jax.shard_map(
        on_device,
        mesh=mesh,
        in_specs=(
            P("gx", "gy", "gz", None, None),
            P("gx", "gy", "gz", None, None),
            P("gx", "gy", "gz", None, None),
            P("gx", "gy", "gz", None),
            P("gx", "gy", "gz", None, None),
            P("gx", "gy", "gz", None, None),
            P("gx", "gy", "gz", None, None),
            P("gx", "gy", "gz", None),
            P("gx", "gy", "gz", None),
            P("gx", "gy", "gz", None),
            P(),
        ),
        out_specs=(
            P("gx", "gy", "gz", None, None),
            P("gx", "gy", "gz", None, None),
            P("gx", "gy", "gz", None, None),
        ),
        check_vma=False,
    )
```

profile of v0, /device:TPU:6, one launch (start us, length us, event | category | flops | bytes accessed | tf_op | source)
XLA Modules:
  0.0 522.4 jit_solution(4546723145671781828)
XLA Ops:
  7.2 2.4 fusion.25
  9.6 2.2 collective-permute-start.2
  11.9 0.8 copy.74
  12.7 0.8 copy.75
  13.5 0.5 collective-permute-start
  14.0 0.6 broadcast.80
  14.6 0.6 reduce.3
  15.8 7.1 %collective-permute-done.2 = f32[2,1,1,120,512]{4,3,1,0,2:T(8,128)} collective-permute-done((f32[2,1,1,120,512]{4,3,1,0,2:T(8,128)}, f32[2,1,1,120,512]{4,3,1,0,2:T(8,128)}, u32[]{:S(2)}, u32[]{:S(2)}) %collective-permute-start.2) | collective-permute-done | bytes 491552 | tf_op jit(solution)/shard_map/ppermute | solution.py:16
  22.9 1.2 collective-permute-done.3
  24.1 1.5 fusion.3
  25.6 0.2 slice_bitcast_fusion.3
  25.9 1.1 copy-done.6
  27.0 1.5 maximum_add_fusion
  28.5 0.2 fusion.23
  28.7 0.6 pad_maximum_fusion
  29.3 0.3 copy-done.9
  29.7 0.5 fusion.7
  30.2 1.0 copy-done.2
  31.2 1.7 fusion.8
  33.0 153.5 %all-reduce.4.cloned.1.call-done = f32[512,512]{1,0:T(8,128)} async-done(((f32[512,512]{1,0:T(8,128)}), f32[512,512]{1,0:T(8,128)}) %all-reduce.4.cloned.1.call-update) | async-done | bytes 1048592 | tf_op jit(solution)/shard_map/psum | solution.py:75
  186.5 2.8 convolution_bitcast_fusion
  189.4 148.8 %all-reduce.6.cloned.1.call-done = f32[512,512]{0,1:T(8,128)} async-done(((f32[512,512]{0,1:T(8,128)}), f32[512,512]{0,1:T(8,128)}) %all-reduce.6.cloned.1.call-update) | async-done | bytes 1048592 | tf_op jit(solution)/shard_map/psum | solution.py:83
  338.5 0.7 fusion.15
  339.2 64.1 %all-reduce.8.cloned.1.call-done = f32[512,512]{0,1:T(8,128)} async-done(((f32[512,512]{0,1:T(8,128)}), f32[512,512]{0,1:T(8,128)}) %all-reduce.8.cloned.1.call-update) | async-done | bytes 1048592 | tf_op jit(solution)/shard_map/psum | solution.py:84
  403.3 3.4 fusion.26
  406.7 1.6 fusion.5
  408.4 78.2 %all-gather.2.cloned.1.call-done = f32[512,512]{1,0:T(8,128)} async-done(((f32[16,512]{1,0:T(8,128)}), f32[512,512]{1,0:T(8,128)}) %all-gather.2.cloned.1.call-update) | async-done | bytes 1048592 | tf_op jit(solution)/shard_map/all_gather | solution.py:87
  486.6 2.0 convolution_convert_fusion
  488.6 0.7 fusion.27
  489.3 1.4 copy-done.3
  490.7 1.3 convolution_add_fusion
  492.0 0.3 copy_multiply_fusion
  492.6 0.5 collective-permute-start.4
  493.1 0.4 slice_bitcast_fusion.6
  493.7 0.6 collective-permute-start.6
  494.4 1.5 collective-permute-start.7
  495.9 0.3 maximum_add_fusion.2
  496.2 1.3 copy.68
  497.6 9.4 %collective-permute-done.6 = f32[2,1,1,120,512]{4,3,0,2,1:T(8,128)S(1)} collective-permute-done((f32[2,1,1,120,512]{4,3,0,2,1:T(8,128)S(1)}, f32[2,1,1,120,512]{4,3,0,2,1:T(8,128)S(1)}, u32[]{:S(2)}, u32[]{:S(2)}) %collective-permute-start.6) | collective-permute-done | bytes 491552 | tf_op jit(solution)/shard_map/ppermute | solution.py:16
  507.0 1.5 collective-permute-done.7
  508.6 0.3 maximum_add_fusion.4
  508.9 0.2 slice_bitcast_fusion.1
  509.2 0.6 pad_maximum_fusion.1
  509.7 0.6 copy.67
  510.3 1.0 copy-done.7
  511.3 2.5 fusion.2
  513.8 1.5 fusion.4
  515.3 0.6 copy-done.1
  (56 shorter events, 1.8 us)
Async XLA Ops:
  7.2 482.1 %copy-start = (bf16[2,2,1,480,480]{4,3,2,1,0:T(8,128)(2,1)S(1)}, bf16[2,2,1,480,480]{4,3,2,1,0:T(8,128)(2,1)}, u32[]{:S(2)}) copy-start(bf16[2,2,1,480,480]{4,3,2,1,0:T(8,128)(2,1)} %param.15) | copy-start | bytes 5529604
  7.2 4.6 copy-start.5
  7.2 179.3 %all-reduce.4.cloned.1.call-start = ((), (), s32[]{:S(2)}) async-start(), calls=%async_computation | async-start | bytes 2097152 | tf_op jit(solution)/shard_map/psum | solution.py:75
  9.6 13.3 %collective-permute-start.2 = (f32[2,1,1,120,512]{4,3,1,0,2:T(8,128)}, f32[2,1,1,120,512]{4,3,1,0,2:T(8,128)}, u32[]{:S(2)}, u32[]{:S(2)}) collective-permute-start(f32[2,1,1,120,512]{4,3,1,0,2:T(8,128)} %get-tuple-element.35), channel_id=1, source_target_pairs={{0,32},{32,64},{64,96},{96,0},{1,33},{33,65},{65,97},{97,1},{2,34}... | collective-permute-start | bytes 1474568 | tf_op jit(solution)/shard_map/ppermute | solution.py:16
  11.8 12.3 %collective-permute-start.3 = (f32[2,1,1,120,512]{4,3,1,0,2:T(8,128)}, f32[2,1,1,120,512]{4,3,1,0,2:T(8,128)}, u32[]{:S(2)}, u32[]{:S(2)}) collective-permute-start(f32[2,1,1,120,512]{4,3,1,0,2:T(8,128)} %get-tuple-element.36), channel_id=1, source_target_pairs={{32,0},{64,32},{96,64},{0,96},{33,1},{65,33},{97,65},{1,97},{34,2}... | collective-permute-start | bytes 1474568 | tf_op jit(solution)/shard_map/ppermute | solution.py:17
  11.9 2.2 copy-start.13
  11.9 2.7 copy-start.14
  11.9 3.7 copy-start.12
  11.9 12.2 %copy-start.4 = (f32[2,3,1,120,512]{4,3,2,1,0:T(8,128)S(1)}, f32[2,3,1,120,512]{4,3,2,1,0:T(8,128)}, u32[]{:S(2)}) copy-start(f32[2,3,1,120,512]{4,3,2,1,0:T(8,128)} %param.12) | copy-start | bytes 4423684
  12.7 13.1 %collective-permute-start.1 = (f32[1,2,1,120,512]{4,3,0,1,2:T(8,128)}, f32[1,2,1,120,512]{4,3,0,1,2:T(8,128)}, u32[]{:S(2)}, u32[]{:S(2)}) collective-permute-start(f32[1,2,1,120,512]{4,3,0,1,2:T(8,128)} %copy.74), channel_id=1, source_target_pairs={{128,0},{0,128},{129,1},{1,129},{130,2},{2,130},{131,3},{3,131},{1... | collective-permute-start | bytes 1474568 | tf_op jit(solution)/shard_map/ppermute | solution.py:17
  13.5 12.3 %collective-permute-start = (f32[1,2,1,120,512]{4,3,0,1,2:T(8,128)}, f32[1,2,1,120,512]{4,3,0,1,2:T(8,128)}, u32[]{:S(2)}, u32[]{:S(2)}) collective-permute-start(f32[1,2,1,120,512]{4,3,0,1,2:T(8,128)} %copy.75), channel_id=1, source_target_pairs={{0,128},{128,0},{1,129},{129,1},{2,130},{130,2},{3,131},{131,3},{4... | collective-permute-start | bytes 1474568 | tf_op jit(solution)/shard_map/ppermute | solution.py:16
  25.6 1.4 copy-start.6
  28.7 1.0 copy-start.9
  29.3 1.9 copy-start.2
  31.2 155.3 %copy-start.10 = (f32[1,1,16,512]{3,2,1,0:T(8,128)S(1)}, f32[1,1,16,512]{3,2,1,0:T(8,128)}, u32[]{:S(2)}) copy-start(f32[1,1,16,512]{3,2,1,0:T(8,128)} %param.20) | copy-start | bytes 98308
  32.9 305.4 %all-reduce.6.cloned.1.call-start = ((), (), s32[]{:S(2)}) async-start(), calls=%async_computation.1 | async-start | bytes 2097152 | tf_op jit(solution)/shard_map/psum | solution.py:83
  33.0 305.6 %copy-start.11 = (f32[1,1,16,512]{3,2,1,0:T(8,128)S(1)}, f32[1,1,16,512]{3,2,1,0:T(8,128)}, u32[]{:S(2)}) copy-start(f32[1,1,16,512]{3,2,1,0:T(8,128)} %param.19) | copy-start | bytes 98308
  186.5 152.0 %copy-start.8 = (f32[512,512]{1,0:T(8,128)S(1)}, f32[512,512]{1,0:T(8,128)}, u32[]{:S(2)}) copy-start(f32[512,512]{1,0:T(8,128)} %all-reduce.4.cloned.1.call-done) | copy-start | bytes 3145732
  189.4 213.9 %all-reduce.8.cloned.1.call-start = ((), (), s32[]{:S(2)}) async-start(), calls=%async_computation.2 | async-start | bytes 2097152 | tf_op jit(solution)/shard_map/psum | solution.py:84
  338.3 148.3 %all-gather.2.cloned.1.call-start = ((), (), s32[]{:S(2)}) async-start(), calls=%async_computation.3 | async-start | bytes 1081344 | tf_op jit(solution)/shard_map/all_gather | solution.py:87
  488.5 2.1 copy-start.3
  492.5 3.3 collective-permute-start.5
  492.6 3.2 collective-permute-start.4
  493.7 13.3 %collective-permute-start.6 = (f32[2,1,1,120,512]{4,3,0,2,1:T(8,128)S(1)}, f32[2,1,1,120,512]{4,3,0,2,1:T(8,128)S(1)}, u32[]{:S(2)}, u32[]{:S(2)}) collective-permute-start(f32[2,1,1,120,512]{4,3,0,2,1:T(8,128)S(1)} %get-tuple-element.27), channel_id=1, source_target_pairs={{0,32},{32,64},{64,96},{96,0},{1,33},{33,65},{65,97},{97,1},{2,34}... | collective-permute-start | bytes 1474568 | tf_op jit(solution)/shard_map/ppermute | solution.py:16
  494.4 14.2 %collective-permute-start.7 = (f32[2,1,1,120,512]{4,3,0,2,1:T(8,128)S(1)}, f32[2,1,1,120,512]{4,3,0,2,1:T(8,128)S(1)}, u32[]{:S(2)}, u32[]{:S(2)}) collective-permute-start(f32[2,1,1,120,512]{4,3,0,2,1:T(8,128)S(1)} %get-tuple-element.28), channel_id=1, source_target_pairs={{32,0},{64,32},{96,64},{0,96},{33,1},{65,33},{97,65},{1,97},{34,2}... | collective-permute-start | bytes 1474568 | tf_op jit(solution)/shard_map/ppermute | solution.py:17
  509.7 1.5 copy-start.7
  513.8 2.1 copy-start.1
Sparse Core Ops, SparseCore 0:
  33.0 153.4 all-reduce.3
  190.5 147.6 all-reduce.5
  340.6 62.6 all-reduce.7
  408.4 78.0 all-gather.1
where the time goes:
time: 523 us; the launch traced here: 522 us
  waiting for transfers between devices  464 us (89%)
  matrix products  17.2 us (3%)
  between operations  14.1 us (3%)
  local copies, waits for them, and re-layouts  13.3 us (3%)
  other arithmetic  8.02 us (2%)
  starting transfers between devices  5.73 us (1%)
    psum x1, waiting for transfers between devices, on_device(): column_res = lax.psum(column_part, 'gz')  154 us
    psum x1, waiting for transfers between devices, on_device(): column_top = lax.psum(top_part, 'gz')  149 us
    all_gather x1, waiting for transfers between devices, on_device(): column_vals = lax.all_gather(value_rows, 'gz', axis=0, tiled=True)  78.2 us
    psum x1, waiting for transfers between devices, on_device(): top_res = lax.psum(column_top, ('gx', 'gy'))  64.1 us
    ppermute x4, waiting for transfers between devices, with_halo(): before = lax.ppermute(last, axis, up)  16.6 us
  transfers between devices with their start and end apart: 12, of which 8 were waited for; matrix products, arithmetic and copies ran while one was open for 2% of the time, Pallas kernels for 0%

commit v1 on v0

--- a/solution.py
+++ b/solution.py
@@ -84,7 +84,10 @@
     top_res = lax.psum(column_top, ("gx", "gy"))
     level_three = jnp.dot(top_inverse, top_res, precision=high)
     value_rows = level_two + jnp.dot(basis_rows, level_three, precision=high)
-    column_vals = lax.all_gather(value_rows, "gz", axis=0, tiled=True)
+    devices = lax.axis_size("gz")
+    parts = jnp.stack([value_rows for _ in range(devices)])
+    parts = lax.all_to_all(parts, "gz", split_axis=0, concat_axis=0)
+    column_vals = jnp.concatenate(parts, axis=0)
     coarse_vals = (
         jnp.dot(onehot, column_vals, precision=high)
         .reshape(4, coarse_local, loads)

time: 523 us -> 483 us (0.924)
  waiting for transfers between devices: 464 us -> 415 us
  starting transfers between devices: 5.73 us -> 15.5 us
    all_gather x1 -> x0, waiting for transfers between devices: 78.2 us -> none  [on_device(): column_vals = lax.all_gather(value_rows, 'gz', axis=0, tiled=True)]
    all_to_all x0 -> x1, waiting for transfers between devices: none -> 28.8 us  [on_device(): parts = lax.all_to_all(parts, 'gz', split_axis=0, concat_axis=0)]
    all_to_all x0 -> x1, starting transfers between devices: none -> 10 us  [on_device(): parts = lax.all_to_all(parts, 'gz', split_axis=0, concat_axis=0)]
where the time goes in v1:
time: 483 us; the launch traced here: 482 us
  waiting for transfers between devices  415 us (86%)
  starting transfers between devices  15.5 us (3%)
  matrix products  15.4 us (3%)
  local copies, waits for them, and re-layouts  14.4 us (3%)
  between operations  14.1 us (3%)
  other arithmetic  8.02 us (2%)
    psum x1, waiting for transfers between devices, on_device(): column_res = lax.psum(column_part, 'gz')  153 us
    psum x1, waiting for transfers between devices, on_device(): column_top = lax.psum(top_part, 'gz')  149 us
    psum x1, waiting for transfers between devices, on_device(): top_res = lax.psum(column_top, ('gx', 'gy'))  64.3 us
    all_to_all x1, waiting for transfers between devices, on_device(): parts = lax.all_to_all(parts, 'gz', split_axis=0, concat_axis=0)  28.8 us
    ppermute x4, waiting for transfers between devices, with_halo(): before = lax.ppermute(last, axis, up)  16.6 us
    all_to_all x1, starting transfers between devices, on_device(): parts = lax.all_to_all(parts, 'gz', split_axis=0, concat_axis=0)  10 us
  transfers between devices with their start and end apart: 12, of which 8 were waited for; matrix products, arithmetic and copies ran while one was open for 2% of the time, Pallas kernels for 0%

profile of v1, /device:TPU:6, one launch (start us, length us, event | category | flops | bytes accessed | tf_op | source)
XLA Modules:
  0.0 482.1 jit_solution(9640983474781880057)
XLA Ops:
  7.2 2.4 fusion.27
  9.6 2.2 collective-permute-start.2
  11.9 0.8 copy.54
  12.7 0.8 copy.55
  13.5 0.5 collective-permute-start
  14.0 0.5 broadcast.101
  14.6 0.6 reduce.3
  15.7 7.2 %collective-permute-done.2 = f32[2,1,1,120,512]{4,3,1,0,2:T(8,128)} collective-permute-done((f32[2,1,1,120,512]{4,3,1,0,2:T(8,128)}, f32[2,1,1,120,512]{4,3,1,0,2:T(8,128)}, u32[]{:S(2)}, u32[]{:S(2)}) %collective-permute-start.2) | collective-permute-done | bytes 491552 | tf_op jit(solution)/shard_map/ppermute | solution.py:16
  22.9 1.2 collective-permute-done.3
  24.1 1.5 fusion.3
  25.6 0.2 slice_bitcast_fusion.3
  25.9 1.1 copy-done.6
  27.0 1.5 maximum_add_fusion
  28.7 0.6 pad_maximum_fusion
  29.3 0.3 copy-done.9
  29.7 0.5 fusion.7
  30.2 1.0 copy-done.2
  31.2 1.7 fusion.10
  33.0 153.5 %all-reduce.4.cloned.1.call-done = f32[512,512]{1,0:T(8,128)} async-done(((f32[512,512]{1,0:T(8,128)}), f32[512,512]{1,0:T(8,128)}) %all-reduce.4.cloned.1.call-update) | async-done | bytes 1048592 | tf_op jit(solution)/shard_map/psum | solution.py:75
  186.5 2.8 convolution_bitcast_fusion
  189.4 148.8 %all-reduce.6.cloned.1.call-done = f32[512,512]{0,1:T(8,128)} async-done(((f32[512,512]{0,1:T(8,128)}), f32[512,512]{0,1:T(8,128)}) %all-reduce.6.cloned.1.call-update) | async-done | bytes 1048592 | tf_op jit(solution)/shard_map/psum | solution.py:83
  338.3 0.7 fusion.17
  338.9 64.3 %all-reduce.8.cloned.1.call-done = f32[512,512]{0,1:T(8,128)} async-done(((f32[512,512]{0,1:T(8,128)}), f32[512,512]{0,1:T(8,128)}) %all-reduce.8.cloned.1.call-update) | async-done | bytes 1048592 | tf_op jit(solution)/shard_map/psum | solution.py:84
  403.2 3.4 fusion.28
  406.6 1.0 fusion.5
  407.6 1.1 stack.46
  408.7 10.0 %all-to-all-start = ((f32[32,16,512]{2,1,0:T(8,128)}), f32[32,16,512]{2,1,0:T(8,128)S(1)}, u32[]{:S(2)}, u32[]{:S(2)}) async-start(f32[32,16,512]{2,1,0:T(8,128)} %stack.46), calls=%async_computation | async-start | bytes 2097152 | tf_op jit(solution)/shard_map/all_to_all | solution.py:89
  418.9 28.8 %all-to-all-done = f32[32,16,512]{2,1,0:T(8,128)S(1)} async-done(((f32[32,16,512]{2,1,0:T(8,128)}), f32[32,16,512]{2,1,0:T(8,128)S(1)}, u32[]{:S(2)}, u32[]{:S(2)}) %all-to-all-start) | async-done | bytes 1048608 | tf_op jit(solution)/shard_map/all_to_all | solution.py:89
  447.7 0.7 convolution_convert_fusion
  448.4 0.7 fusion.29
  449.2 1.4 copy-done.3
  450.5 1.3 convolution_add_fusion
  451.9 0.3 copy_multiply_fusion
  452.5 0.5 collective-permute-start.4
  453.0 0.4 slice_bitcast_fusion.6
  453.7 2.0 collective-permute-start.7
  455.7 0.3 maximum_add_fusion.2
  456.0 1.3 copy.48
  457.5 9.4 %collective-permute-done.6 = f32[2,1,1,120,512]{4,3,0,2,1:T(8,128)S(1)} collective-permute-done((f32[2,1,1,120,512]{4,3,0,2,1:T(8,128)S(1)}, f32[2,1,1,120,512]{4,3,0,2,1:T(8,128)S(1)}, u32[]{:S(2)}, u32[]{:S(2)}) %collective-permute-start.6) | collective-permute-done | bytes 491552 | tf_op jit(solution)/shard_map/ppermute | solution.py:16
  466.9 1.3 collective-permute-done.7
  468.2 0.3 maximum_add_fusion.4
  468.5 0.2 slice_bitcast_fusion.1
  468.8 0.6 pad_maximum_fusion.1
  469.4 0.6 copy.47
  470.0 1.0 copy-done.7
  470.9 2.5 fusion.2
  473.5 1.5 fusion.4
  474.9 0.6 copy-done.1
  (56 shorter events, 1.8 us)
Async XLA Ops:
  7.2 442.0 %copy-start = (bf16[2,2,1,480,480]{4,3,2,1,0:T(8,128)(2,1)S(1)}, bf16[2,2,1,480,480]{4,3,2,1,0:T(8,128)(2,1)}, u32[]{:S(2)}) copy-start(bf16[2,2,1,480,480]{4,3,2,1,0:T(8,128)(2,1)} %param.15) | copy-start | bytes 5529604
  7.2 4.6 copy-start.5
  7.2 179.3 %all-reduce.4.cloned.1.call-start = ((), (), s32[]{:S(2)}) async-start(), calls=%async_computation.1 | async-start | bytes 2097152 | tf_op jit(solution)/shard_map/psum | solution.py:75
  9.6 13.3 %collective-permute-start.2 = (f32[2,1,1,120,512]{4,3,1,0,2:T(8,128)}, f32[2,1,1,120,512]{4,3,1,0,2:T(8,128)}, u32[]{:S(2)}, u32[]{:S(2)}) collective-permute-start(f32[2,1,1,120,512]{4,3,1,0,2:T(8,128)} %get-tuple-element.32), channel_id=1, source_target_pairs={{0,32},{32,64},{64,96},{96,0},{1,33},{33,65},{65,97},{97,1},{2,34}... | collective-permute-start | bytes 1474568 | tf_op jit(solution)/shard_map/ppermute | solution.py:16
  11.8 12.3 %collective-permute-start.3 = (f32[2,1,1,120,512]{4,3,1,0,2:T(8,128)}, f32[2,1,1,120,512]{4,3,1,0,2:T(8,128)}, u32[]{:S(2)}, u32[]{:S(2)}) collective-permute-start(f32[2,1,1,120,512]{4,3,1,0,2:T(8,128)} %get-tuple-element.33), channel_id=1, source_target_pairs={{32,0},{64,32},{96,64},{0,96},{33,1},{65,33},{97,65},{1,97},{34,2}... | collective-permute-start | bytes 1474568 | tf_op jit(solution)/shard_map/ppermute | solution.py:17
  11.9 2.2 copy-start.14
  11.9 2.7 copy-start.13
  11.9 3.7 copy-start.12
  11.9 12.2 %copy-start.4 = (f32[2,3,1,120,512]{4,3,2,1,0:T(8,128)S(1)}, f32[2,3,1,120,512]{4,3,2,1,0:T(8,128)}, u32[]{:S(2)}) copy-start(f32[2,3,1,120,512]{4,3,2,1,0:T(8,128)} %param.12) | copy-start | bytes 4423684
  12.7 13.1 %collective-permute-start.1 = (f32[1,2,1,120,512]{4,3,0,1,2:T(8,128)}, f32[1,2,1,120,512]{4,3,0,1,2:T(8,128)}, u32[]{:S(2)}, u32[]{:S(2)}) collective-permute-start(f32[1,2,1,120,512]{4,3,0,1,2:T(8,128)} %copy.54), channel_id=1, source_target_pairs={{128,0},{0,128},{129,1},{1,129},{130,2},{2,130},{131,3},{3,131},{1... | collective-permute-start | bytes 1474568 | tf_op jit(solution)/shard_map/ppermute | solution.py:17
  13.5 12.3 %collective-permute-start = (f32[1,2,1,120,512]{4,3,0,1,2:T(8,128)}, f32[1,2,1,120,512]{4,3,0,1,2:T(8,128)}, u32[]{:S(2)}, u32[]{:S(2)}) collective-permute-start(f32[1,2,1,120,512]{4,3,0,1,2:T(8,128)} %copy.55), channel_id=1, source_target_pairs={{0,128},{128,0},{1,129},{129,1},{2,130},{130,2},{3,131},{131,3},{4... | collective-permute-start | bytes 1474568 | tf_op jit(solution)/shard_map/ppermute | solution.py:16
  25.6 1.4 copy-start.6
  28.7 1.0 copy-start.9
  29.3 1.9 copy-start.2
  31.2 155.3 %copy-start.10 = (f32[1,1,16,512]{3,2,1,0:T(8,128)S(1)}, f32[1,1,16,512]{3,2,1,0:T(8,128)}, u32[]{:S(2)}) copy-start(f32[1,1,16,512]{3,2,1,0:T(8,128)} %param.20) | copy-start | bytes 98308
  32.9 305.3 %all-reduce.6.cloned.1.call-start = ((), (), s32[]{:S(2)}) async-start(), calls=%async_computation.2 | async-start | bytes 2097152 | tf_op jit(solution)/shard_map/psum | solution.py:83
  33.0 305.3 %copy-start.11 = (f32[1,1,16,512]{3,2,1,0:T(8,128)S(1)}, f32[1,1,16,512]{3,2,1,0:T(8,128)}, u32[]{:S(2)}) copy-start(f32[1,1,16,512]{3,2,1,0:T(8,128)} %param.19) | copy-start | bytes 98308
  186.5 151.8 %copy-start.8 = (f32[512,512]{1,0:T(8,128)S(1)}, f32[512,512]{1,0:T(8,128)}, u32[]{:S(2)}) copy-start(f32[512,512]{1,0:T(8,128)} %all-reduce.4.cloned.1.call-done) | copy-start | bytes 3145732
  189.3 213.9 %all-reduce.8.cloned.1.call-start = ((), (), s32[]{:S(2)}) async-start(), calls=%async_computation.3 | async-start | bytes 2097152 | tf_op jit(solution)/shard_map/psum | solution.py:84
  408.7 38.9 %all-to-all-start = ((f32[32,16,512]{2,1,0:T(8,128)}), f32[32,16,512]{2,1,0:T(8,128)S(1)}, u32[]{:S(2)}, u32[]{:S(2)}) async-start(f32[32,16,512]{2,1,0:T(8,128)} %stack.46), calls=%async_computation | async-start | bytes 2097152 | tf_op jit(solution)/shard_map/all_to_all | solution.py:89
  448.4 2.1 copy-start.3
  452.4 3.3 collective-permute-start.5
  452.5 3.2 collective-permute-start.4
  453.6 13.3 %collective-permute-start.6 = (f32[2,1,1,120,512]{4,3,0,2,1:T(8,128)S(1)}, f32[2,1,1,120,512]{4,3,0,2,1:T(8,128)S(1)}, u32[]{:S(2)}, u32[]{:S(2)}) collective-permute-start(f32[2,1,1,120,512]{4,3,0,2,1:T(8,128)S(1)} %get-tuple-element.24), channel_id=1, source_target_pairs={{0,32},{32,64},{64,96},{96,0},{1,33},{33,65},{65,97},{97,1},{2,34}... | collective-permute-start | bytes 1474568 | tf_op jit(solution)/shard_map/ppermute | solution.py:16
  453.7 14.5 %collective-permute-start.7 = (f32[2,1,1,120,512]{4,3,0,2,1:T(8,128)S(1)}, f32[2,1,1,120,512]{4,3,0,2,1:T(8,128)S(1)}, u32[]{:S(2)}, u32[]{:S(2)}) collective-permute-start(f32[2,1,1,120,512]{4,3,0,2,1:T(8,128)S(1)} %get-tuple-element.25), channel_id=1, source_target_pairs={{32,0},{64,32},{96,64},{0,96},{33,1},{65,33},{97,65},{1,97},{34,2}... | collective-permute-start | bytes 1474568 | tf_op jit(solution)/shard_map/ppermute | solution.py:17
  469.4 1.5 copy-start.7
  473.5 2.1 copy-start.1
Sparse Core Ops, SparseCore 0:
  33.0 153.3 all-reduce.3
  190.5 147.6 all-reduce.5
  340.6 62.6 all-reduce.7
